TPU v7x, 128 devices: a whole 4x4x4 slice. The times are simulated.
128 devices in a mesh: req: 16 (over x, y), head: 8 (over z, core).
Axes of the slice: x: 4, y: 4, z: 4, core: 2. Of those that a mesh axis runs over, the one named last changes fastest.
Arguments:
- hidden: bfloat16 [4096, 2048], P('req'), may hold values from -6 to 6
- attn_gain: float32 [2048], replicated, may hold values from 0.1 to 1.9
- attn_router: float32 [2048, 4], replicated, may hold values from -8 to 8
- attention_expert_pairs: int32 [4096, 2], P('req'), may hold values from 0 to 3, all different within a row
- key_value_weight: bfloat16 [2, 2048, 2048], P(None, None, 'head'), may hold values from -0.125 to 0.125
- query_weight: bfloat16 [4, 2048, 2048], P(None, None, 'head'), may hold values from -0.125 to 0.125
- output_weight: bfloat16 [4, 2048, 2048], P(None, 'head'), may hold values from -0.125 to 0.125
- paged_key_value_cache: bfloat16 [2, 512, 128, 2048], P(None, 'req', None, 'head'), may hold values from -70 to 70
- page_table: int32 [64, 30], P('req'), may hold values from 0 to 29, as said below
- cache_len: int32 [64], P('req'), may hold values from 1 to 3312, as said below
- ancestor: int32 [64, 64, 64], P('req'), may hold values from 0 to 1, as said below
- ffn_gain: float32 [2048], replicated, may hold values from 0.1 to 1.9
- ffn_router: float32 [2048, 8], replicated, may hold values from -8 to 8
- ffn_route: int32 [4096, 2], P('req'), may hold values from 0 to 7, all different within a row; in each aligned block of 256 rows (0 to 255, 256 to 511, ...) at most 96 rows name the same one
- w_gate_up: bfloat16 [8, 2, 5632, 2048], P('head', None, 'req'), may hold values from -0.125 to 0.125
- w_down: bfloat16 [8, 5632, 2048], P('head', 'req'), may hold values from -0.078125 to 0.078125
- accept_path: int32 [64, 16], P('req'), may hold values from 0 to 30, as said below
- accept_count: int32 [64], P('req'), may hold values from 1 to 16
- mig_slot: int32 [16], P('req'), may hold values from 0 to 3, as said below
- destination: int32 [16], replicated, may hold values from 0 to 15, as said below
Outputs:
- layer_out: bfloat16 [4096, 2048], P(('req', 'head'))
- kv_out: bfloat16 [2, 512, 128, 2048], P(None, 'req', None, 'head')
Inputs may be any that keep to these rules, and one draw needn't show every extreme that they name: `page_table`: with n_i = ceil((cache_len[i] + 16) / 128), entries j < n_i of row i are distinct slots below 30, unlike those of the other requests of the same row of requests, and the n_i of one row sum to exactly 30; later entries are 0 and unused. `cache_len`: one request of each row holds most of the row's pages; the largest value is reached in some row. ancestor[i, a, b] = 1 exactly where b is a or an ancestor of a in request i's tree; a token's parent has a lower index, one or two below its own, and token 0 is the root. For t < accept_count[i], accept_path[i, t] is the token of depth t on one path from the root of request i's tree; later entries are 0. `mig_slot`: the moving request has exactly 2 pages. `destination`: A permutation of the rows in which no row maps to itself. `ffn_route`: in the 256 rows of one index of req no expert is named by more than 96 rows; the entries of a row differ. `attention_expert_pairs`: the entries of a row differ.
All inputs are finite; a program needn't handle non-finite values.
Results may differ from a plain program's by a relative error of at most 0.023.
Values may be sent and summed in bfloat16 or wider, within the bound.
A program may use at most 128 MiB of HBM per device.

v0:
```python
import math

import jax
import jax.numpy as jnp
from jax import lax
from jax.sharding import PartitionSpec as P

HEAD_SIZE = 128
DRAFT = 64
PAGE_POSITIONS = 128
MIGP = 2
PAGES = 32
CAP = 96


EPS = 1e-06
NEG = -1e30


def rms_scale(values, norm_gain):
    mean_sq = jnp.mean(values * values, axis=-1, keepdims=True)
    return values * lax.rsqrt(mean_sq + EPS) * norm_gain


def pair_gates(logits, route_ids):
    picked = jnp.take_along_axis(logits, route_ids, axis=1)
    top_value = jnp.max(picked, axis=1, keepdims=True)
    exp_terms = jnp.exp(picked - top_value)
    return exp_terms / jnp.sum(exp_terms, axis=1, keepdims=True)


def rotate(values, position):
    half_size = values.shape[-1] // 2
    frequency = jnp.exp(
        jnp.arange(half_size).astype(jnp.float32) * (-2.0 * math.log(10000.0) / values.shape[-1])
    )
    angles = position.astype(jnp.float32)[:, None] * frequency[None, :]
    table_shape = (values.shape[0],) + (1,) * (values.ndim - 2) + (half_size,)
    cosine = jnp.cos(angles).reshape(table_shape)
    sine_part = jnp.sin(angles).reshape(table_shape)
    first_half = values[..., :half_size]
    second_half = values[..., half_size:]
    return jnp.concatenate(
        [
            first_half * cosine - second_half * sine_part,
            second_half * cosine + first_half * sine_part,
        ],
        axis=-1,
    )


def on_device(
    hidden,
    attn_gain,
    attn_router,
    attention_expert_pairs,
    key_value_weight,
    query_weight,
    output_weight,
    paged_key_value_cache,
    page_table,
    cache_len,
    ancestor,
    ffn_gain,
    ffn_router,
    ffn_route,
    w_gate_up,
    w_down,
    accept_path,
    accept_count,
    mig_slot,
    destination,
):
    tok_rows = hidden.shape[0]
    col_width = key_value_weight.shape[2]
    heads_here = col_width // HEAD_SIZE
    experts_here = w_down.shape[0]
    requests_here = cache_len.shape[0]
    table_width = page_table.shape[1]
    num_rows = lax.axis_size("req")
    num_groups = lax.axis_size("head")
    row_index = lax.axis_index("req")
    group_index = lax.axis_index("head")
    own_share = tok_rows // num_groups
    score_scale = 1.0 / math.sqrt(HEAD_SIZE)
    stream = hidden.astype(jnp.float32)
    normalized_input = rms_scale(stream, attn_gain).astype(jnp.bfloat16)
    logits = jnp.dot(
        normalized_input.astype(jnp.float32), attn_router, precision=lax.Precision.HIGHEST
    )
    attn_weights = pair_gates(logits, attention_expert_pairs)
    tree_depth = jnp.sum(ancestor, axis=2) - 1
    position = (cache_len[:, None] + tree_depth).reshape(tok_rows)
    projected = jnp.einsum(
        "td,cdh->cth", normalized_input, key_value_weight, preferred_element_type=jnp.float32
    )
    draft_keys = rotate(projected[0].reshape(tok_rows, heads_here, HEAD_SIZE), position).astype(
        jnp.bfloat16
    )
    fresh_value_rows = projected[1].astype(jnp.bfloat16).reshape(tok_rows, heads_here, HEAD_SIZE)
    query_rows_full = jnp.einsum(
        "td,edh->teh", normalized_input, query_weight, preferred_element_type=jnp.float32
    )
    selected_expert = jnp.take_along_axis(
        query_rows_full, attention_expert_pairs[:, :, None], axis=1
    ).reshape(tok_rows, 2, heads_here, HEAD_SIZE)
    queries = rotate(selected_expert, position).astype(jnp.bfloat16)
    entry_ids = jnp.arange(table_width, dtype=jnp.int32)
    live_pages = entry_ids[None, :] * PAGE_POSITIONS < cache_len[:, None]
    target = jnp.where(live_pages, page_table, PAGES).reshape(-1)
    owner_ids = jnp.broadcast_to(
        jnp.arange(requests_here, dtype=jnp.int32)[:, None], live_pages.shape
    ).reshape(-1)
    entry_base = jnp.broadcast_to(entry_ids[None, :] * PAGE_POSITIONS, live_pages.shape).reshape(-1)
    page_owner = jnp.full((PAGES,), -1, jnp.int32).at[target].set(owner_ids, mode="drop")
    page_base = jnp.zeros((PAGES,), jnp.int32).at[target].set(entry_base, mode="drop")
    key_owner = jnp.repeat(page_owner, PAGE_POSITIONS)
    key_pos = (page_base[:, None] + jnp.arange(PAGE_POSITIONS, dtype=jnp.int32)[None, :]).reshape(
        -1
    )
    token_request = jnp.arange(tok_rows, dtype=jnp.int32) // DRAFT
    length_of = cache_len[token_request]
    valid_cache = (key_owner[None, :] == token_request[:, None]) & (
        key_pos[None, :] < length_of[:, None]
    )
    tree_rows = ancestor.reshape(tok_rows, DRAFT)
    valid_draft = (token_request[:, None] == token_request[None, :]) & (
        jnp.tile(tree_rows, (1, requests_here)) > 0
    )
    valid_cache = jnp.repeat(valid_cache, 2, axis=0)
    valid_draft = jnp.repeat(valid_draft, 2, axis=0)
    outputs = []
    for head_num in range(heads_here):
        col_start = head_num * HEAD_SIZE
        query_block = queries[:, :, head_num, :].reshape(tok_rows * 2, HEAD_SIZE)
        stored_key_rows = paged_key_value_cache[0, :, :, col_start : col_start + HEAD_SIZE].reshape(
            PAGES * PAGE_POSITIONS, HEAD_SIZE
        )
        stored_value_rows = paged_key_value_cache[
            1, :, :, col_start : col_start + HEAD_SIZE
        ].reshape(PAGES * PAGE_POSITIONS, HEAD_SIZE)
        score_c = (
            lax.dot_general(
                query_block,
                stored_key_rows,
                (((1,), (1,)), ((), ())),
                preferred_element_type=jnp.float32,
            )
            * score_scale
        )
        score_d = (
            lax.dot_general(
                query_block,
                draft_keys[:, head_num, :],
                (((1,), (1,)), ((), ())),
                preferred_element_type=jnp.float32,
            )
            * score_scale
        )
        score_c = jnp.where(valid_cache, score_c, NEG)
        score_d = jnp.where(valid_draft, score_d, NEG)
        top_value = jnp.maximum(
            jnp.max(score_c, axis=1, keepdims=True), jnp.max(score_d, axis=1, keepdims=True)
        )
        exp_c = jnp.where(valid_cache, jnp.exp(score_c - top_value), 0.0)
        exp_d = jnp.where(valid_draft, jnp.exp(score_d - top_value), 0.0)
        all_terms = jnp.sum(exp_c, axis=1, keepdims=True) + jnp.sum(exp_d, axis=1, keepdims=True)
        prob_c = (exp_c / all_terms).astype(jnp.bfloat16)
        prob_d = (exp_d / all_terms).astype(jnp.bfloat16)
        head_out = jnp.dot(prob_c, stored_value_rows, preferred_element_type=jnp.float32) + jnp.dot(
            prob_d, fresh_value_rows[:, head_num, :], preferred_element_type=jnp.float32
        )
        outputs.append(head_out.reshape(tok_rows, 2, HEAD_SIZE))
    attended = jnp.stack(outputs, axis=2).reshape(tok_rows, 2, col_width)
    gated_out = attended * attn_weights[:, :, None]
    picked_expert = (
        attention_expert_pairs[:, :, None]
        == jnp.arange(query_weight.shape[0], dtype=jnp.int32)[None, None, :]
    )
    mixed = jnp.sum(
        jnp.where(picked_expert[:, :, :, None], gated_out[:, :, None, :], 0.0), axis=1
    ).astype(jnp.bfloat16)
    attn_part = jnp.einsum("teh,ehd->td", mixed, output_weight, preferred_element_type=jnp.float32)
    attn_sum = lax.psum(attn_part, "head")
    resid = (stream + attn_sum).astype(jnp.bfloat16)
    normed_ffn = rms_scale(resid.astype(jnp.float32), ffn_gain).astype(jnp.bfloat16)
    resid_own = lax.dynamic_slice_in_dim(resid, group_index * own_share, own_share, 0)
    ffn_logits = jnp.dot(
        normed_ffn.astype(jnp.float32), ffn_router, precision=lax.Precision.HIGHEST
    )
    ffn_weights = pair_gates(ffn_logits, ffn_route)
    all_experts = ffn_router.shape[1]
    member = jnp.any(
        ffn_route[:, :, None] == jnp.arange(all_experts, dtype=jnp.int32)[None, None, :], axis=1
    ).astype(jnp.int32)
    slot_rank = jnp.cumsum(member, axis=0) - member
    first_expert = group_index * experts_here
    member_here = lax.dynamic_slice_in_dim(member, first_expert, experts_here, 1)
    rank_here = lax.dynamic_slice_in_dim(slot_rank, first_expert, experts_here, 1)
    slot_ids = jnp.arange(CAP, dtype=jnp.int32)
    dispatch = (rank_here[None, :, :] == slot_ids[:, None, None]) & (member_here[None, :, :] > 0)
    outbound = jnp.einsum(
        "cte,td->ced", dispatch.astype(jnp.bfloat16), normed_ffn, preferred_element_type=jnp.float32
    ).astype(jnp.bfloat16)
    gate_up = jnp.einsum(
        "ced,ekfd->kcef",
        lax.all_gather(outbound, "req", axis=0, tiled=True),
        w_gate_up,
        preferred_element_type=jnp.float32,
    )
    hidden_units = (jax.nn.silu(gate_up[0]) * gate_up[1]).astype(jnp.bfloat16)
    partial_all = jnp.einsum(
        "cef,efd->ced", hidden_units, w_down, preferred_element_type=jnp.float32
    )
    all_sums = lax.psum(partial_all.astype(jnp.bfloat16), "req").astype(jnp.float32)
    expert_sum = lax.dynamic_slice_in_dim(all_sums, row_index * CAP, CAP, 0)
    expert_out = expert_sum.astype(jnp.bfloat16)
    chosen_here = (
        ffn_route[:, :, None]
        == (first_expert + jnp.arange(experts_here, dtype=jnp.int32))[None, None, :]
    )
    weight_here = jnp.sum(jnp.where(chosen_here, ffn_weights[:, :, None], 0.0), axis=1)
    combine = jnp.where(dispatch, weight_here[None, :, :], 0.0)
    ffn_part = jnp.einsum(
        "cte,ced->td", combine, expert_out.astype(jnp.float32), precision=lax.Precision.HIGHEST
    )
    ffn_own = lax.psum_scatter(
        ffn_part.astype(jnp.bfloat16), "head", scatter_dimension=0, tiled=True
    ).astype(jnp.float32)
    layer_out = (resid_own.astype(jnp.float32) + ffn_own).astype(jnp.bfloat16)
    flat_pool = paged_key_value_cache.reshape(2, PAGES * PAGE_POSITIONS, col_width)
    step_ids = jnp.arange(accept_path.shape[1], dtype=jnp.int32)
    places = cache_len[:, None] + step_ids[None, :]
    page_slot = jnp.take_along_axis(page_table, places // PAGE_POSITIONS, axis=1)
    flat_index = jnp.where(
        step_ids[None, :] < accept_count[:, None],
        page_slot * PAGE_POSITIONS + places % PAGE_POSITIONS,
        PAGES * PAGE_POSITIONS,
    )
    source = (jnp.arange(requests_here, dtype=jnp.int32)[:, None] * DRAFT + accept_path).reshape(-1)
    fresh_rows = jnp.stack(
        [
            draft_keys.reshape(tok_rows, col_width)[source],
            fresh_value_rows.reshape(tok_rows, col_width)[source],
        ]
    )
    flat_pool = flat_pool.at[:, flat_index.reshape(-1)].set(fresh_rows, mode="drop")
    new_pool = flat_pool.reshape(2, PAGES, PAGE_POSITIONS, col_width)
    moving_req = mig_slot[0]
    moving_pages = lax.dynamic_index_in_dim(page_table, moving_req, 0, keepdims=False)[:MIGP]
    mover_block = new_pool[:, moving_pages]
    target_row = destination[row_index]
    dest_mask = jnp.arange(num_rows, dtype=jnp.int32) == target_row
    outgoing = jnp.where(
        dest_mask[:, None, None, None, None], mover_block[None], jnp.zeros((), jnp.bfloat16)
    )
    arrived = lax.all_to_all(outgoing, "req", split_axis=0, concat_axis=0, tiled=True)
    sender = jnp.argmax(destination == row_index)
    incoming = lax.dynamic_index_in_dim(arrived, sender, 0, keepdims=False)
    new_pool = lax.dynamic_update_slice_in_dim(new_pool, incoming, PAGES - MIGP, 1)
    return (layer_out, new_pool)


def solution(mesh):
    return jax.shard_map(
        on_device,
        mesh=mesh,
        in_specs=(
            P("req", None),
            P(),
            P(),
            P("req", None),
            P(None, None, "head"),
            P(None, None, "head"),
            P(None, "head", None),
            P(None, "req", None, "head"),
            P("req", None),
            P("req"),
            P("req", None, None),
            P(),
            P(),
            P("req", None),
            P("head", None, "req", None),
            P("head", "req", None),
            P("req", None),
            P("req"),
            P("req"),
            P(),
        ),
        out_specs=(P(("req", "head"), None), P(None, "req", None, "head")),
        check_vma=False,
    )
```

profile of v0, /device:TPU:1, one launch (start us, length us, event | category | flops | bytes accessed | tf_op | source)
XLA Modules:
  0.0 482.9 jit_solution(14256673754835841002)
XLA Ops:
  8.9 1.5 fusion.17
  10.4 2.9 convolution_bitcast_fusion.1
  16.4 2.2 fusion.92
  18.6 4.9 %gather_fusion.4 = f32[512]{0:T(512)S(1)} fusion(f32[256,4]{0,1:T(4,128)S(1)} %fusion.92, s32[512]{0:T(512)S(1)} %reshape.962), kind=kCustom, calls=%fused_computation.4 | custom fusion | bytes 8192 | tf_op jit(solution)/shard_map/jit(take_along_axis)/gather | solution.py:26
  25.1 3.8 fusion.27
  28.9 1.6 copy.149
  30.6 6.2 %gather_fusion.3 = f32[512,256]{1,0:T(8,128)S(1)} fusion(f32[256,4,256]{2,1,0:T(4,128)} %copy.149, s32[512]{0:T(512)S(1)} %reshape.962), kind=kCustom, calls=%fused_computation.3 | custom fusion | bytes 1052672 | tf_op jit(solution)/shard_map/jit(take_along_axis)/gather | solution.py:104
  36.8 1.1 gather.34
  41.9 4.4 fusion.97
  47.7 1.2 scatter_custom_fusion
  49.0 2.6 compare_select_fusion.4
  52.5 5.7 %broadcast_in_dim.111 = pred[256,2,4096]{2,1,0:T(4,128)(4,1)} broadcast(pred[256,4096]{1,0:T(8,128)(4,1)S(1)} %compare_and_fusion), dimensions={0,2} | broadcast | bytes 3145728 | tf_op jit(solution)/shard_map/broadcast_in_dim | solution.py:130
  58.2 12.5 %reshape.913 = pred[512,4096]{1,0:T(32,128)(4,1)} reshape(pred[256,2,4096]{2,1,0:T(4,128)(4,1)} %broadcast_in_dim.111) | data formatting | bytes 4194304 | tf_op jit(solution)/shard_map/reshape | solution.py:130
  70.7 1.7 multiply_subtract_fusion
  75.2 2.0 reshape.914
  77.2 1.1 copy.156
  78.3 1.3 copy_select_fusion
  79.7 1.7 subtract_convert_fusion
  82.2 1.3 fusion.102
  84.1 3.8 fusion
  88.0 5.9 %fusion.5 = (f32[512]{0:T(512)S(1)}, f32[512]{0:T(512)}) fusion(pred[512,4096]{1,0:T(32,128)(4,1)S(1)} %copy-done.3, f32[512,4096]{1,0:T(8,128)S(1)} %get-tuple-element.34, f32[512]{0:T(512)S(1)} %max.16, f32[512]{0:T(512)S(1)} %max.17, f32[512,4096]{1,0:T(8,128)S(1)} %fusion.102), kind=kLoop, calls=%fused_computation.22 | loop fusion | flops 20970496 | bytes 18882560 | tf_op jit(solution)/shard_map/reduce_sum | solution.py:167
  94.7 3.6 fusion.7
  98.3 1.0 convolution_add_fusion.1
  99.3 1.8 copy.160
  101.8 20.4 %fusion.8 = f32[512,128]{1,0:T(8,128)S(1)} fusion(bf16[4096,128]{1,0:T(8,128)(2,1)} %bitcast.161, pred[512,4096]{1,0:T(32,128)(4,1)} %reshape.913, f32[512,4096]{1,0:T(8,128)} %copy-done.2, f32[512]{0:T(512)S(1)} %add.358, f32[512]{0:T(512)} %copy-done.19), kind=kOutput, calls=%fused_computation.27 | convolution fusion | flops 549453824 | bytes 11800576 | tf_op jit(solution)/shard_map/dot_general | solution.py:170
  123.3 1.1 copy.161
  127.8 1.5 select_reduce_fusion
  129.4 4.8 convolution_bitcast_fusion
  135.2 66.4 %all-reduce.3.cloned.1.call-done = f32[256,2048]{1,0:T(8,128)} async-done(((f32[256,2048]{1,0:T(8,128)}), f32[256,2048]{1,0:T(8,128)}) %all-reduce.3.cloned.1.call-update) | async-done | bytes 2097168 | tf_op jit(solution)/shard_map/psum | solution.py:184
  201.6 2.2 fusion.14
  203.8 1.1 copy-done.7
  204.9 1.2 convolution_convert_fusion.2
  206.2 62.4 %all-gather.3.cloned.1.call-done = bf16[1536,2048]{1,0:T(8,128)(2,1)} async-done(((bf16[96,2048]{1,0:T(8,128)(2,1)}), bf16[1536,2048]{1,0:T(8,128)(2,1)}) %all-gather.3.cloned.1.call-update) | async-done | bytes 6291472 | tf_op jit(solution)/shard_map/all_gather | solution.py:207
  268.6 6.9 %fusion.9 = f32[2,1536,1,352]{1,3,0,2:T(8,128)S(1)} fusion(bf16[1536,2048]{1,0:T(8,128)(2,1)} %all-gather.3.cloned.1.call-done, bf16[1,2,352,2048]{3,2,1,0:T(8,128)(2,1)S(1)} %copy-done), kind=kOutput, calls=%fused_computation.28 | convolution fusion | flops 4429185024 | bytes 13500416 | tf_op jit(solution)/shard_map/ced,ekfd->kcef/dot_general | solution.py:205
  275.6 5.4 %fusion.2 = bf16[1536,1,2048]{2,0,1:T(8,128)(2,1)} fusion(bf16[1,352,2048]{2,1,0:T(8,128)(2,1)S(1)} %copy-done.29, f32[2,1536,1,352]{1,3,0,2:T(8,128)S(1)} %fusion.9), kind=kOutput, calls=%fused_computation.19 | convolution fusion | flops 2220982272 | bytes 12058624 | tf_op jit(solution)/shard_map/cef,efd->ced/dot_general | solution.py:212
  281.1 8.7 %copy.166 = bf16[2,32,128,256]{3,0,2,1:T(2,128)(2,1)} copy(bf16[2,32,128,256]{3,2,1,0:T(8,128)(2,1)} %param.27) | data formatting | bytes 8388608 | tf_op args[7]
  294.8 7.5 %scatter_fusion = bf16[2,4096,256]{2,0,1:T(2,128)(2,1)} fusion(bf16[2,4096,256]{2,0,1:T(2,128)(2,1)} %bitcast.149, s32[64]{0:T(128)S(1)} %get-tuple-element.41, bf16[64,2,256]{2,1,0:T(2,128)(2,1)S(1)} %copy.169), kind=kCustom, calls=%fused_computation.9 | custom fusion | bytes 196864 | tf_op jit(solution)/shard_map/scatter | solution.py:247
  302.4 3.3 gather_fusion.2
  307.0 2.3 broadcast_select_fusion
  309.3 5.6 %all-to-all-start = ((bf16[16,2,2,128,256]{4,3,2,1,0:T(8,128)(2,1)}), bf16[16,2,2,128,256]{4,3,2,1,0:T(8,128)(2,1)}, u32[]{:S(2)}, u32[]{:S(2)}) async-start(bf16[16,2,2,128,256]{4,3,2,1,0:T(8,128)(2,1)} %broadcast_select_fusion), calls=%async_computation.1 | async-start | bytes 8388608 | tf_op jit(solution)/shard_map/all_to_all | solution.py:257
  315.3 2.2 fusion.36
  317.5 3.5 gather_fusion.5
  321.3 120.5 %all-reduce.5.cloned.1.call-done = bf16[1536,1,2048]{2,0,1:T(8,128)(2,1)} async-done(((bf16[1536,1,2048]{2,0,1:T(8,128)(2,1)}), bf16[1536,1,2048]{2,0,1:T(8,128)(2,1)}) %all-reduce.5.cloned.1.call-update) | async-done | bytes 6291472 | tf_op jit(solution)/shard_map/psum | solution.py:215
  441.8 3.0 convolution_convert_fusion.1
  444.9 5.1 %copy.171 = bf16[2,32,128,256]{3,2,1,0:T(8,128)(2,1)} copy(bf16[2,32,128,256]{3,0,2,1:T(2,128)(2,1)} %bitcast.151) | data formatting | bytes 8388608 | tf_op jit(solution)/shard_map/reshape | solution.py:248
  452.4 1.7 bitcast_dynamic-update-slice_fusion
  454.1 20.4 %reduce-scatter.2.cloned.1.call-done = bf16[32,2048]{1,0:T(8,128)(2,1)} async-done(((bf16[256,2048]{1,0:T(8,128)(2,1)}), bf16[32,2048]{1,0:T(8,128)(2,1)}) %reduce-scatter.2.cloned.1.call-update) | async-done | bytes 131088 | tf_op jit(solution)/shard_map/reduce_scatter | solution.py:227
  474.5 1.7 add_convert_fusion.1
  (174 shorter events, 30.9 us)
Async XLA Ops:
  7.2 261.5 %copy-start = (bf16[1,2,352,2048]{3,2,1,0:T(8,128)(2,1)S(1)}, bf16[1,2,352,2048]{3,2,1,0:T(8,128)(2,1)}, u32[]{:S(2)}) copy-start(bf16[1,2,352,2048]{3,2,1,0:T(8,128)(2,1)} %param.34) | copy-start | bytes 8650756
  7.2 9.2 %copy-start.32 = (f32[2048]{0:T(1024)S(1)}, f32[2048]{0:T(1024)}, u32[]{:S(2)}) copy-start(f32[2048]{0:T(1024)} %param.21) | copy-start | bytes 24580
  7.2 7.7 %copy-start.21 = (s32[256,2]{0,1:T(2,128)S(1)}, s32[256,2]{0,1:T(2,128)}, u32[]{:S(2)}) copy-start(s32[256,2]{0,1:T(2,128)} %param.23) | copy-start | bytes 6148
  7.2 8.3 %copy-start.18 = (s32[256,2]{0,1:T(2,128)S(1)}, s32[256,2]{0,1:T(2,128)}, u32[]{:S(2)}) copy-start(s32[256,2]{0,1:T(2,128)} %param.33) | copy-start | bytes 6148
  7.2 9.2 %copy-start.31 = (f32[2048,4]{0,1:T(4,128)S(1)}, f32[2048,4]{0,1:T(4,128)}, u32[]{:S(2)}) copy-start(f32[2048,4]{0,1:T(4,128)} %param.22) | copy-start | bytes 98308
  7.2 194.4 %all-reduce.3.cloned.1.call-start = ((), (), s32[]{:S(2)}) async-start(), calls=%async_computation.2 | async-start | bytes 4194304 | tf_op jit(solution)/shard_map/psum | solution.py:184
  13.4 0.9 copy-start.12
  24.3 4.6 copy-start.22
  28.9 9.0 %copy-start.11 = (s32[4,64,64]{2,1,0:T(8,128)S(1)}, s32[4,64,64]{2,1,0:T(8,128)}, u32[]{:S(2)}) copy-start(s32[4,64,64]{2,1,0:T(8,128)} %param.30) | copy-start | bytes 196612
  28.9 9.7 %copy-start.17 = (s32[4]{0:T(128)S(1)}, s32[4]{0:T(128)}, u32[]{:S(2)}) copy-start(s32[4]{0:T(128)} %param.29) | copy-start | bytes 52
  41.9 4.4 copy-start.1
  41.9 4.4 copy-start.25
  41.9 9.6 %copy-start.23 = (s32[256]{0:T(256)S(1)}, s32[256]{0:T(256)}, u32[]{:S(2)}) copy-start(s32[256]{0:T(256)} %and_select_fusion.5) | copy-start | bytes 3076
  58.2 20.1 %copy-start.6 = (f32[256,2,2,128]{3,2,1,0:T(2,128)S(1)}, f32[256,2,2,128]{3,2,1,0:T(2,128)}, u32[]{:S(2)}) copy-start(f32[256,2,2,128]{3,2,1,0:T(2,128)} %gather.34) | copy-start | bytes 1572868
  77.2 4.9 %copy-start.5 = (bf16[1,32,128,128]{3,2,1,0:T(8,128)(2,1)S(1)}, bf16[1,32,128,128]{3,2,1,0:T(8,128)(2,1)}, u32[]{:S(2)}) copy-start(bf16[1,32,128,128]{3,2,1,0:T(8,128)(2,1)} %get-tuple-element.17) | copy-start | bytes 3145732
  82.1 1.3 copy-start.13
  82.1 1.3 copy-start.14
  82.2 1.9 copy-start.3
  82.2 1.9 copy-start.4
  83.4 4.5 copy-start.2
  83.5 4.4 copy-start.8
  87.9 5.9 %copy-start.19 = (f32[512]{0:T(512)}, f32[512]{0:T(512)S(1)}, u32[]{:S(2)}) copy-start(f32[512]{0:T(512)S(1)} %max.17) | copy-start | bytes 6148
  88.0 6.7 %copy-start.10 = (bf16[1,32,128,128]{3,2,1,0:T(8,128)(2,1)S(1)}, bf16[1,32,128,128]{3,2,1,0:T(8,128)(2,1)}, u32[]{:S(2)}) copy-start(bf16[1,32,128,128]{3,2,1,0:T(8,128)(2,1)} %get-tuple-element.16) | copy-start | bytes 3145732
  94.7 3.6 copy-start.15
  101.8 20.4 %copy-start.16 = (bf16[1,256,256]{1,2,0:T(8,128)(2,1)S(1)}, bf16[1,256,256]{1,2,0:T(8,128)(2,1)}, u32[]{:S(2)}) copy-start(bf16[1,256,256]{1,2,0:T(8,128)(2,1)} %slice.157) | copy-start | bytes 393220
  101.8 20.4 %copy-start.20 = (f32[512]{0:T(512)S(1)}, f32[512]{0:T(512)}, u32[]{:S(2)}) copy-start(f32[512]{0:T(512)} %copy-done.19) | copy-start | bytes 6148
  134.1 70.8 %copy-start.33 = (f32[2048]{0:T(1024)S(1)}, f32[2048]{0:T(1024)}, u32[]{:S(2)}) copy-start(f32[2048]{0:T(1024)} %param.31) | copy-start | bytes 24580
  134.2 134.5 %all-gather.3.cloned.1.call-start = ((), (), s32[]{:S(2)}) async-start(), calls=%async_computation.5 | async-start | bytes 6684672 | tf_op jit(solution)/shard_map/all_gather | solution.py:207
  203.8 1.1 copy-start.7
  206.2 235.6 %all-reduce.5.cloned.1.call-start = ((), (), s32[]{:S(2)}) async-start(), calls=%async_computation.3 | async-start | bytes 12582912 | tf_op jit(solution)/shard_map/psum | solution.py:215
  268.6 6.9 %copy-start.29 = (bf16[1,352,2048]{2,1,0:T(8,128)(2,1)S(1)}, bf16[1,352,2048]{2,1,0:T(8,128)(2,1)}, u32[]{:S(2)}) copy-start(bf16[1,352,2048]{2,1,0:T(8,128)(2,1)} %param.35) | copy-start | bytes 4325380
  281.0 8.7 %copy-start.9 = (bf16[256,2,128]{0,2,1:T(8,128)(2,1)S(1)}, bf16[256,2,128]{0,2,1:T(8,128)(2,1)}, u32[]{:S(2)}) copy-start(bf16[256,2,128]{0,2,1:T(8,128)(2,1)} %copy-done.8) | copy-start | bytes 393220
  281.0 9.9 %copy-start.26 = (s32[4,16]{1,0:T(4,128)S(1)}, s32[4,16]{1,0:T(4,128)}, u32[]{:S(2)}) copy-start(s32[4,16]{1,0:T(4,128)} %param.36) | copy-start | bytes 772
  281.0 10.3 %copy-start.27 = (s32[4]{0:T(128)S(1)}, s32[4]{0:T(128)}, u32[]{:S(2)}) copy-start(s32[4]{0:T(128)} %param.37) | copy-start | bytes 52
  289.7 16.0 %copy-start.28 = (s32[16]{0:T(128)S(1)}, s32[16]{0:T(128)}, u32[]{:S(2)}) copy-start(s32[16]{0:T(128)} %param.39) | copy-start | bytes 196
  309.2 5.7 %copy-start.24 = (s32[256,2,1]{0,1,2:T(2,128)S(1)}, s32[256,2,1]{0,1,2:T(2,128)}, u32[]{:S(2)}) copy-start(s32[256,2,1]{0,1,2:T(2,128)} %get-tuple-element.39) | copy-start | bytes 6148
  309.2 6.0 %copy-start.30 = (f32[2048,8]{0,1:T(8,128)S(1)}, f32[2048,8]{0,1:T(8,128)}, u32[]{:S(2)}) copy-start(f32[2048,8]{0,1:T(8,128)} %param.32) | copy-start | bytes 196612
  309.3 143.2 %all-to-all-start = ((bf16[16,2,2,128,256]{4,3,2,1,0:T(8,128)(2,1)}), bf16[16,2,2,128,256]{4,3,2,1,0:T(8,128)(2,1)}, u32[]{:S(2)}, u32[]{:S(2)}) async-start(bf16[16,2,2,128,256]{4,3,2,1,0:T(8,128)(2,1)} %broadcast_select_fusion), calls=%async_computation.1 | async-start | bytes 8388608 | tf_op jit(solution)/shard_map/all_to_all | solution.py:257
  314.9 159.6 %reduce-scatter.2.cloned.1.call-start = ((), (), s32[]{:S(2)}) async-start(), calls=%async_computation.4 | async-start | bytes 1179648 | tf_op jit(solution)/shard_map/reduce_scatter | solution.py:227
Sparse Core Ops, SparseCore 0:
  134.3 67.2 all-reduce.2
  206.3 62.3 all-gather.2
  281.1 160.6 all-reduce.4
  445.0 29.4 reduce-scatter.1
where the time goes:
time: 486 us; the launch traced here: 483 us
  waiting for transfers between devices  270 us (56%)
  local copies, waits for them, and re-layouts  89.2 us (18%)
  matrix products  64.3 us (13%)
  other arithmetic  36.7 us (8%)
  between operations  17.2 us (4%)
  starting transfers between devices  5.81 us (1%)
    psum x1, waiting for transfers between devices, on_device(): lax.psum(partial_all.astype(jnp.bfloat16), 'req').astype(jnp.float32)  120 us
    psum x1, waiting for transfers between devices, on_device(): attn_sum = lax.psum(attn_part, 'head')  66.4 us
    all_gather x1, waiting for transfers between devices, on_device(): lax.all_gather(outbound, 'req', axis=0, tiled=True)  62.4 us
    dot_general x2, matrix products, on_device(): jnp.dot(prob_c, stored_value_rows, preferred_element_type=jnp.float32)  24 us
    reduce_scatter x1, waiting for transfers between devices, on_device(): lax.psum_scatter(ffn_part.astype(jnp.bfloat16), 'head', scatter_dimension...  20.4 us
    reshape x1, local copies, waits for them, and re-layouts, on_device(): valid_cache = jnp.repeat(valid_cache, 2, axis=0)  12.5 us
    unnamed x69, local copies, waits for them, and re-layouts  9.99 us
  transfers between devices with their start and end apart: 5, of which 4 were waited for; matrix products, arithmetic and copies ran while one was open for 9% of the time, Pallas kernels for 0%

commit v1 on v0

v1 whole, which is shorter than its diff:
```python
import math

import jax
import jax.numpy as jnp
from jax import lax
from jax.experimental import pallas as pl
from jax.experimental.pallas import tpu as pltpu
from jax.sharding import PartitionSpec as P

EPS = 1e-06
NEG = -1e30
BF16 = jnp.bfloat16
F32 = jnp.float32
MESH = pl.DeviceIdType.MESH
ENTRIES = 30
CAP = 96
QUARTER = 512
HALF = 1024


def dot_nn(a, b):
    return lax.dot_general(a, b, (((1,), (0,)), ((), ())), preferred_element_type=F32)


def dot_nt(a, b):
    return lax.dot_general(a, b, (((1,), (1,)), ((), ())), preferred_element_type=F32)


def iota(shape, axis):
    return lax.broadcasted_iota(jnp.int32, shape, axis)


def split_dot(rows, weights):
    high = weights.astype(BF16)
    rest = weights - high.astype(F32)
    middle = rest.astype(BF16)
    low = (rest - middle.astype(F32)).astype(BF16)
    return dot_nt(rows, high) + dot_nt(rows, middle) + dot_nt(rows, low)


def as_columns(rows):
    n = rows.shape[1]
    eye = (iota((n, n), 0) == iota((n, n), 1)).astype(F32).astype(BF16)
    return dot_nt(eye, rows.astype(F32).astype(BF16))


def pair_gates(logits, columns):
    lanes = iota(logits.shape, 1).astype(F32)
    picked = [
        jnp.sum(jnp.where(lanes == columns[:, s : s + 1], logits, 0.0), axis=1, keepdims=True)
        for s in range(2)
    ]
    top = jnp.maximum(picked[0], picked[1])
    terms = [jnp.exp(value - top) for value in picked]
    total = terms[0] + terms[1]
    return [term / total for term in terms]


def attend_kernel(
    len_s,
    table_s,
    count_s,
    mig_s,
    hidden_r,
    gain_r,
    router_r,
    pairs_r,
    anc_r,
    path_r,
    route_r,
    kvw_h,
    qw_h,
    ow_h,
    pool_h,
    part_r,
    mover_r,
    disp_r,
    dispt_r,
    out_h,
    wbuf,
    owbuf,
    pool,
    norm_v,
    cos_v,
    sin_v,
    qsel,
    q_v,
    kd,
    vd,
    scores,
    peak,
    acc,
    mix,
    ent_page,
    ent_req,
    ent_cnt,
    sems,
):
    loads = []
    for c in range(2):
        loads.append(pltpu.make_async_copy(kvw_h.at[c], wbuf.at[c], sems.at[c]))
    for c in range(4):
        loads.append(pltpu.make_async_copy(qw_h.at[c], wbuf.at[2 + c], sems.at[2 + c]))
    for c in range(2):
        loads.append(pltpu.make_async_copy(pool_h.at[c], pool.at[c], sems.at[6 + c]))
    loads.append(pltpu.make_async_copy(ow_h, owbuf, sems.at[8]))
    for load in loads:
        load.start()

    offset = jnp.int32(0)
    for i in range(4):
        length = len_s[i]
        pages = (length + (16 + 127)) // 128

        def add_entry(j, carry, i=i, length=length, offset=offset):
            e = offset + j
            ent_page[e] = table_s[i, j]
            ent_req[e] = jnp.int32(i)
            ent_cnt[e] = jnp.clip(length - j * 128, 0, 128)
            return carry

        lax.fori_loop(0, pages, add_entry, 0)
        offset = offset + pages

    gain = gain_r[...]

    def norm_rows(j, carry):
        rows = pl.ds(pl.multiple_of(j * 32, 32), 32)
        x = hidden_r[rows, :].astype(F32)
        mean_sq = jnp.mean(x * x, axis=1, keepdims=True)
        norm_v[rows, :] = (x * lax.rsqrt(mean_sq + EPS) * gain).astype(BF16)
        return carry

    lax.fori_loop(0, 8, norm_rows, 0)

    lane = iota((64, 128), 1)
    entry = jnp.where(lane >= 64, lane - 64, lane).astype(F32)
    frequency = jnp.exp(entry * (-2.0 * math.log(10000.0) / 128))
    for i in range(4):
        depth = jnp.sum(anc_r[i].astype(F32), axis=1, keepdims=True) - 1.0
        angles = (depth + len_s[i].astype(F32)) * frequency
        cos_v[i * 64 : (i + 1) * 64, :] = jnp.cos(angles)
        sine = jnp.sin(angles)
        sin_v[i * 64 : (i + 1) * 64, :] = jnp.where(lane < 64, -sine, sine)

    def rotate(values, i):
        rows = slice(i * 64, (i + 1) * 64)
        return values * cos_v[rows, :] + pltpu.roll(values, 64, 1) * sin_v[rows, :]

    pair_cols = as_columns(pairs_r[...])
    gates = pair_gates(split_dot(norm_v[...], router_r[...]), pair_cols)

    zeros = jnp.zeros((64, 256), BF16)
    loads[0].wait()
    proj = dot_nn(norm_v[...], wbuf[0])
    for i in range(4):
        for h in range(2):
            cols = slice(h * 128, (h + 1) * 128)
            kd[i, 0:64, cols] = rotate(proj[i * 64 : (i + 1) * 64, cols], i).astype(BF16)
        kd[i, 64:128, :] = zeros
    loads[1].wait()
    proj = dot_nn(norm_v[...], wbuf[1])
    for i in range(4):
        vd[i, 0:64, :] = proj[i * 64 : (i + 1) * 64, :].astype(BF16)
        vd[i, 64:128, :] = zeros

    for e in range(4):
        loads[2 + e].wait()
        proj = dot_nn(norm_v[...], wbuf[2 + e])
        for s in range(2):
            if e == 0:
                qsel[s] = proj
            else:
                qsel[s] = jnp.where(pair_cols[:, s : s + 1] == float(e), proj, qsel[s])
    for i in range(4):
        for s in range(2):
            for h in range(2):
                picked = qsel[s, i * 64 : (i + 1) * 64, h * 128 : (h + 1) * 128]
                q_v[h, i, s * 64 : (s + 1) * 64, :] = rotate(picked, i).astype(BF16)

    scale = 1.0 / math.sqrt(128)
    wide = iota((128, 128), 1)
    for i in range(4):
        tree = anc_r[i].astype(F32)
        for h in range(2):
            cols = slice(h * 128, (h + 1) * 128)
            score = dot_nt(q_v[h, i], kd[i, 0:64, cols]) * scale
            for s in range(2):
                rows = slice(s * 64, (s + 1) * 64)
                masked = jnp.where(tree > 0.0, score[rows, :], NEG)
                scores[h, ENTRIES + i, rows, 0:64] = masked
                peak[h, i, rows, 0:64] = masked
            scores[h, ENTRIES + i, :, 64:128] = jnp.full((128, 64), NEG, F32)
            peak[h, i, :, 64:128] = jnp.full((128, 64), NEG, F32)
    loads[6].wait()

    def score_entries(step, carry):
        for k in range(5):
            e = step * 5 + k
            page, i, count = ent_page[e], ent_req[e], ent_cnt[e]
            keys = pool[0, page]
            for h in range(2):
                score = dot_nt(q_v[h, i], keys[:, h * 128 : (h + 1) * 128]) * scale
                score = jnp.where(wide < count, score, NEG)
                scores[h, e] = score
                peak[h, i] = jnp.maximum(peak[h, i], score)
        return carry

    lax.fori_loop(0, ENTRIES // 5, score_entries, 0)

    ones = jnp.ones((128, 128), BF16)
    loads[7].wait()
    for i in range(4):
        for h in range(2):
            top = jnp.broadcast_to(jnp.max(peak[h, i], axis=1, keepdims=True), (128, 128))
            peak[h, i] = top
            terms = jnp.exp(scores[h, ENTRIES + i] - top).astype(BF16)
            values = jnp.concatenate([vd[i, :, h * 128 : (h + 1) * 128], ones], axis=1)
            acc[h, i] = dot_nn(terms, values)

    def sum_entries(step, carry):
        for k in range(5):
            e = step * 5 + k
            page, i = ent_page[e], ent_req[e]
            page_values = pool[1, page]
            for h in range(2):
                terms = jnp.exp(scores[h, e] - peak[h, i]).astype(BF16)
                values = jnp.concatenate([page_values[:, h * 128 : (h + 1) * 128], ones], axis=1)
                acc[h, i] += dot_nn(terms, values)
        return carry

    lax.fori_loop(0, ENTRIES // 5, sum_entries, 0)

    place = iota((128, 16), 0)
    step_ids = iota((128, 16), 1)
    tokens = iota((128, 64), 1).astype(F32)
    for i in range(4):
        length, count = len_s[i], count_s[i]
        first = length // 128
        path = path_r[i : i + 1, :].astype(F32)
        for extra in range(2):
            spot = first + extra
            page = table_s[i, jnp.minimum(spot, ENTRIES - 1)]
            hit = (place + (spot * 128 - length) == step_ids) & (step_ids < count)
            taken = jnp.sum(jnp.where(hit, 1.0, 0.0), axis=1, keepdims=True)
            token = jnp.sum(jnp.where(hit, path, 0.0), axis=1, keepdims=True)
            token = jnp.where(taken > 0.0, token, -1.0)
            choose = jnp.where(tokens == token, 1.0, 0.0).astype(BF16)
            for which, fresh in ((0, kd), (1, vd)):
                new = dot_nn(choose, fresh[i, 0:64, :])
                old = pool[which, page].astype(F32)
                pool[which, page] = jnp.where(taken > 0.0, new, old).astype(BF16)
    moving = mig_s[0]
    for which in range(2):
        for j in range(2):
            mover_r[which, j] = pool[which, table_s[moving, j]]
    stores = [
        pltpu.make_async_copy(
            pool.at[which, pl.ds(0, ENTRIES)], out_h.at[which, pl.ds(0, ENTRIES)], sems.at[9 + which]
        )
        for which in range(2)
    ]
    for store in stores:
        store.start()

    for i in range(4):
        rows = slice(i * 64, (i + 1) * 64)
        for h in range(2):
            total = acc[h, i]
            attended = total[:, 0:128] / total[:, 128:256]
            gated = [attended[s * 64 : (s + 1) * 64, :] * gates[s][rows, :] for s in range(2)]
            for e in range(4):
                mixed = jnp.where(pair_cols[rows, 0:1] == float(e), gated[0], 0.0) + jnp.where(
                    pair_cols[rows, 1:2] == float(e), gated[1], 0.0
                )
                mix[rows, e * 256 + h * 128 : e * 256 + (h + 1) * 128] = mixed.astype(BF16)

    expert = lax.axis_index("head")
    route = route_r[...]
    named = jnp.where(route == expert, 1.0, 0.0)
    member = named[0:1, :] + named[1:2, :]
    before = (iota((256, 256), 0) < iota((256, 256), 1)).astype(F32).astype(BF16)
    rank = dot_nn(jnp.broadcast_to(member, (8, 256)).astype(BF16), before)[0:1, :]
    slots = iota((CAP, 256), 0).astype(F32)
    chosen = jnp.where(slots == rank, 1.0, 0.0) * member
    disp_r[...] = chosen.astype(BF16)
    eye = (iota((256, 256), 0) == iota((256, 256), 1)).astype(F32).astype(BF16)
    dispt_r[...] = dot_nt(eye, chosen.astype(BF16)).astype(BF16)

    loads[8].wait()
    for n in range(4):
        cols = slice(n * QUARTER, (n + 1) * QUARTER)
        out = dot_nn(mix[:, 0:256], owbuf[0, :, cols])
        for e in range(1, 4):
            out = out + dot_nn(mix[:, e * 256 : (e + 1) * 256], owbuf[e, :, cols])
        for b in range(8):
            part_r[b % 2, b // 2, :, cols] = out[b * 32 : (b + 1) * 32, :].astype(BF16)
    for store in stores:
        store.wait()


def attend(args):
    vmem = pl.BlockSpec(memory_space=pltpu.VMEM)
    smem = pl.BlockSpec(memory_space=pltpu.SMEM)
    anywhere = pl.BlockSpec(memory_space=pl.ANY)
    return pl.pallas_call(
        attend_kernel,
        out_shape=(
            jax.ShapeDtypeStruct((2, 4, 32, 2048), BF16),
            jax.ShapeDtypeStruct((2, 2, 128, 256), BF16),
            jax.ShapeDtypeStruct((CAP, 256), BF16),
            jax.ShapeDtypeStruct((256, CAP), BF16),
            jax.ShapeDtypeStruct((2, 32, 128, 256), BF16),
        ),
        in_specs=[smem] * 4 + [vmem] * 7 + [anywhere] * 4,
        out_specs=(vmem, vmem, vmem, vmem, anywhere),
        scratch_shapes=[
            pltpu.VMEM((6, 2048, 256), BF16),
            pltpu.VMEM((4, 256, 2048), BF16),
            pltpu.VMEM((2, 32, 128, 256), BF16),
            pltpu.VMEM((256, 2048), BF16),
            pltpu.VMEM((256, 128), F32),
            pltpu.VMEM((256, 128), F32),
            pltpu.VMEM((2, 256, 256), F32),
            pltpu.VMEM((2, 4, 128, 128), BF16),
            pltpu.VMEM((4, 128, 256), BF16),
            pltpu.VMEM((4, 128, 256), BF16),
            pltpu.VMEM((2, ENTRIES + 4, 128, 128), F32),
            pltpu.VMEM((2, 4, 128, 128), F32),
            pltpu.VMEM((2, 4, 128, 256), F32),
            pltpu.VMEM((256, 1024), BF16),
            pltpu.SMEM((32,), jnp.int32),
            pltpu.SMEM((32,), jnp.int32),
            pltpu.SMEM((32,), jnp.int32),
            pltpu.SemaphoreType.DMA((11,)),
        ],
        name="attend",
    )(*args)


def greet(devices):
    barrier = pltpu.get_barrier_semaphore()
    for device in devices:
        pl.semaphore_signal(barrier, inc=1, device_id=device, device_id_type=MESH)
    pl.semaphore_wait(barrier, len(devices))


class Sender:
    def __init__(self, send_sems, recv_sems):
        self.send_sems, self.recv_sems = send_sems, recv_sems
        self.copies = {}

    def send(self, index, src, dst, device):
        copy = pltpu.make_async_remote_copy(
            src_ref=src,
            dst_ref=dst,
            send_sem=self.send_sems.at[index],
            recv_sem=self.recv_sems.at[index],
            device_id=device,
            device_id_type=MESH,
        )
        copy.start()
        self.copies[index] = copy

    def arrived(self, index):
        self.copies[index].wait_recv()

    def drain(self):
        for copy in self.copies.values():
            copy.wait_send()


def head_place():
    h = lax.axis_index("head")
    z, core = h // 2, lax.rem(h, 2)

    def along(step):
        return {"head": lax.rem(z + (step + 4), 4) * 2 + core}

    return h, z, core, along, {"head": z * 2 + (1 - core)}


def reduce_over_head(own, got, relay, near, far, sent, sender, base):
    h, z, core, along, partner = head_place()
    order = (2, 1, 3, 0)
    for k, step in enumerate(order):
        zz = lax.rem(z + step, 4)
        sender.send(base + k, own.at[1 - core, zz], got.at[zz], partner)

    def columns(q):
        return pl.ds(q * HALF, HALF)

    for k, step in enumerate(order):
        zz = lax.rem(z + step, 4)
        sender.arrived(base + k)
        sent[step] = (own[core, zz].astype(F32) + got[zz].astype(F32)).astype(BF16)
        if step == 2:
            for q, s in ((0, 1), (1, -1)):
                sender.send(base + 4 + q, sent.at[2, :, columns(q)], relay.at[q], along(s))
        if step == 1:
            sender.send(base + 6 + 1, sent.at[1, :, columns(1)], near.at[1], along(1))
        if step == 3:
            sender.send(base + 6, sent.at[3, :, columns(0)], near.at[0], along(-1))
    for q, s in ((0, 1), (1, -1)):
        sender.arrived(base + 4 + q)
        passed = relay[q].astype(F32) + sent[s % 4, :, columns(q)].astype(F32)
        sent[s % 4, :, columns(q)] = passed.astype(BF16)
        sender.send(base + 8 + q, sent.at[s % 4, :, columns(q)], far.at[q], along(s))
    halves = []
    for q in range(2):
        sender.arrived(base + 6 + q)
        sender.arrived(base + 8 + q)
        halves.append(
            sent[0, :, columns(q)].astype(F32) + near[q].astype(F32) + far[q].astype(F32)
        )
    return halves


HEAD_SCRATCH = [
    pltpu.VMEM((4, 32, 2048), BF16),
    pltpu.VMEM((2, 32, HALF), BF16),
    pltpu.VMEM((2, 32, HALF), BF16),
    pltpu.VMEM((2, 32, HALF), BF16),
    pltpu.VMEM((4, 32, 2048), BF16),
]


def head_kernel(
    dest_s,
    part_r,
    hidden_r,
    gain_r,
    router_r,
    route_r,
    mover_r,
    disp_r,
    outb_r,
    resid_r,
    gate_r,
    incoming_r,
    got,
    relay,
    near,
    far,
    sent,
    norms,
    mb,
    sb,
    mr,
    send_sems,
    recv_sems,
):
    h, z, core, along, partner = head_place()
    r = lax.axis_index("req")
    x, y = r // 4, lax.rem(r, 4)

    def place(which, u, v):
        return u * 4 + v if which == 0 else v * 4 + u

    def shift(u, step):
        return lax.rem(u + (step + 4), 4)

    spots = ((x, y), (y, x))
    devices = [partner, along(1), along(-1)]
    for which, (u, v) in enumerate(spots):
        devices += [{"req": place(which, shift(u, d), v)} for d in (1, 2, 3)]
    greet(devices)
    sender = Sender(send_sems, recv_sems)

    for which, (u, v) in enumerate(spots):
        for d in (1, 2, 3):
            sender.send(
                24 + which * 3 + d - 1,
                mover_r.at[which],
                mb.at[which, d],
                {"req": place(which, shift(u, d), v)},
            )
        mb[which, 0] = mover_r[which]

    halves = reduce_over_head(part_r, got, relay, near, far, sent, sender, 0)

    rows = pl.ds(pl.multiple_of(h * 32, 32), 32)
    sums = []
    for q in range(2):
        cols = slice(q * HALF, (q + 1) * HALF)
        resid = (hidden_r[rows, cols].astype(F32) + halves[q]).astype(BF16)
        resid_r[:, cols] = resid
        wide = resid.astype(F32)
        sums.append(jnp.sum(wide * wide, axis=1, keepdims=True))
    scale = lax.rsqrt((sums[0] + sums[1]) * (1.0 / 2048) + EPS)
    for q in range(2):
        cols = slice(q * HALF, (q + 1) * HALF)
        norms[h, :, cols] = (resid_r[:, cols].astype(F32) * scale * gain_r[:, cols]).astype(BF16)

    def block(step, q):
        return norms.at[shift(z, step) * 2 + core, :, pl.ds(q * HALF, HALF)]

    turns = ((0, 1), (1, -1))
    for q, s in turns:
        sender.send(10 + q, block(0, q), block(0, q), along(s))
    for q, s in turns:
        sender.send(12 + q, block(0, q), block(0, q), along(-s))
    for q, s in turns:
        sender.send(16 + q, block(0, q), block(0, q), partner)

    for k in range(24, 30):
        sender.arrived(k)
    for which, (u, v) in enumerate(spots):
        for d in (0, 1, 2, 3):
            target = place(which, u, shift(v, d))
            pick = jnp.int32(0)
            for k in (1, 2, 3):
                found = dest_s[place(which, shift(u, -k), v)] == target
                pick = jnp.where(found, jnp.int32(k), pick)
            if d == 0:
                mr[which, 0] = mb[which, pick]
            else:
                sb[which, d - 1] = mb[which, pick]
                sender.send(
                    30 + which * 3 + d - 1, sb.at[which, d - 1], mr.at[which, d], {"req": target}
                )

    for q, s in turns:
        sender.arrived(10 + q)
        sender.send(14 + q, block(-s, q), block(-s, q), along(s))
        sender.send(18 + q, block(-s, q), block(-s, q), partner)
    for q, s in turns:
        sender.arrived(12 + q)
        sender.send(20 + q, block(s, q), block(s, q), partner)
    for q, s in turns:
        sender.arrived(14 + q)
        sender.send(22 + q, block(2, q), block(2, q), partner)
    for k in range(16, 24):
        sender.arrived(k)

    for which in range(2):
        for d in (1, 2, 3):
            sender.arrived(30 + which * 3 + d - 1)
    for which, (u, v) in enumerate(spots):
        back = jnp.int32(0)
        for d in (1, 2, 3):
            for k in range(4):
                found = dest_s[place(which, shift(u, k), shift(v, -d))] == r
                back = jnp.where(found, jnp.int32(d), back)
        incoming_r[which] = mr[which, back]

    normed = norms[...].reshape(256, 2048)
    for q in range(4):
        outb_r[q] = dot_nn(disp_r[...], normed[:, q * QUARTER : (q + 1) * QUARTER]).astype(BF16)
    route_cols = as_columns(route_r[...])
    weights = pair_gates(split_dot(normed, router_r[...]), route_cols)
    expert = h.astype(F32)
    mine = jnp.where(route_cols[:, 0:1] == expert, weights[0], 0.0) + jnp.where(
        route_cols[:, 1:2] == expert, weights[1], 0.0
    )
    gate_r[...] = jnp.broadcast_to(mine, (256, 128))
    sender.drain()


def head_stage(args):
    vmem = pl.BlockSpec(memory_space=pltpu.VMEM)
    smem = pl.BlockSpec(memory_space=pltpu.SMEM)
    return pl.pallas_call(
        head_kernel,
        out_shape=(
            jax.ShapeDtypeStruct((4, CAP, QUARTER), BF16),
            jax.ShapeDtypeStruct((32, 2048), BF16),
            jax.ShapeDtypeStruct((256, 128), F32),
            jax.ShapeDtypeStruct((2, 2, 128, 256), BF16),
        ),
        in_specs=[smem] + [vmem] * 7,
        out_specs=(vmem, vmem, vmem, vmem),
        scratch_shapes=HEAD_SCRATCH
        + [
            pltpu.VMEM((8, 32, 2048), BF16),
            pltpu.VMEM((2, 4, 2, 128, 256), BF16),
            pltpu.VMEM((2, 3, 2, 128, 256), BF16),
            pltpu.VMEM((2, 4, 2, 128, 256), BF16),
            pltpu.SemaphoreType.DMA((36,)),
            pltpu.SemaphoreType.DMA((36,)),
        ],
        compiler_params=pltpu.CompilerParams(collective_id=1, has_side_effects=True),
        name="head_stage",
    )(*args)


TURNS = ((0, 1), (0, -1), (1, 1), (1, -1))
LAST = 60


def ffn_kernel(
    outb_r,
    resid_r,
    gate_r,
    dispt_r,
    wgu_h,
    wd_h,
    layer_r,
    rows_v,
    parts,
    ra,
    rb,
    rc,
    rd,
    re,
    rf,
    wgu,
    wd,
    eo,
    blocks,
    got,
    relay,
    near,
    far,
    sent,
    load_sems,
    send_sems,
    recv_sems,
    back_send,
    back_recv,
    head_send,
    head_recv,
):
    h, z, core, along, partner = head_place()
    r = lax.axis_index("req")
    x, y = r // 4, lax.rem(r, 4)

    def shift(u, step):
        return lax.rem(u + (step + 4), 4)

    def spot(q):
        return (x, y) if TURNS[q][0] == 0 else (y, x)

    def at(q, du, dv):
        u, v = spot(q)
        u, v = shift(u, du), shift(v, dv)
        return u * 4 + v if TURNS[q][0] == 0 else v * 4 + u

    loads = [
        pltpu.make_async_copy(wgu_h, wgu, load_sems.at[0]),
        pltpu.make_async_copy(wd_h, wd, load_sems.at[1]),
    ]
    for load in loads:
        load.start()
    greet(
        [{"req": at(0, d, 0)} for d in (1, -1)]
        + [{"req": at(0, 0, d)} for d in (1, -1)]
        + [partner, along(1), along(-1)]
    )

    sender = Sender(send_sems, recv_sems)

    def pass_on(q, message, du, dv, step_u, step_v):
        here = rows_v.at[q, at(q, du, dv)]
        sender.send(q * 15 + message, here, here, {"req": at(q, step_u, step_v)})

    for q in range(4):
        rows_v[q, r] = outb_r[q]
    for q, (_, s) in enumerate(TURNS):
        pass_on(q, 0, 0, 0, s, 0)
        pass_on(q, 1, 0, 0, -s, 0)
    for q, (_, s) in enumerate(TURNS):
        pass_on(q, 3, 0, 0, 0, s)
        pass_on(q, 4, 0, 0, 0, -s)

    def offset(k, s):
        return (0, -s, s, 2)[k]

    def spread(q, k, s):
        pass_on(q, 3 + 3 * k, offset(k, s), 0, 0, s)
        pass_on(q, 4 + 3 * k, offset(k, s), 0, 0, -s)

    def forward(q, k, s):
        sender.arrived(q * 15 + 3 + 3 * k)
        pass_on(q, 5 + 3 * k, offset(k, s), -s, 0, s)

    for q, (_, s) in enumerate(TURNS):
        sender.arrived(q * 15)
        pass_on(q, 2, -s, 0, s, 0)
        spread(q, 1, s)
    for q, (_, s) in enumerate(TURNS):
        sender.arrived(q * 15 + 1)
        spread(q, 2, s)
    for q, (_, s) in enumerate(TURNS):
        forward(q, 0, s)
    for q, (_, s) in enumerate(TURNS):
        sender.arrived(q * 15 + 2)
        spread(q, 3, s)
    for k in (1, 2, 3):
        for q, (_, s) in enumerate(TURNS):
            forward(q, k, s)
    for k in range(4):
        for q in range(4):
            sender.arrived(q * 15 + 4 + 3 * k)
            sender.arrived(q * 15 + 5 + 3 * k)

    for load in loads:
        load.wait()

    def some_rows(j, carry):
        group = pl.ds(j * 4, 4)
        gate = jnp.zeros((4 * CAP, 352), F32)
        up = jnp.zeros((4 * CAP, 352), F32)
        for q in range(4):
            held = rows_v[q, group].reshape(4 * CAP, QUARTER)
            cols = slice(q * QUARTER, (q + 1) * QUARTER)
            gate = gate + dot_nt(held, wgu[0, :, cols])
            up = up + dot_nt(held, wgu[1, :, cols])
        units = (jax.nn.silu(gate) * up).astype(BF16)
        for q in range(4):
            out = dot_nn(units, wd[:, q * QUARTER : (q + 1) * QUARTER])
            parts[q, group] = out.astype(BF16).reshape(4, CAP, QUARTER)
        return carry

    lax.fori_loop(0, 4, some_rows, 0)

    back = Sender(back_send, back_recv)

    def add(q, du, dv, *others):
        block = at(q, du, dv)
        total = parts[q, block].astype(F32)
        for other in others:
            total = total + other.astype(F32)
        parts[q, block] = total.astype(BF16)

    def turn_order(s):
        return (2, (-s) % 4, s % 4, 0)

    for place in range(4):
        for q, (_, s) in enumerate(TURNS):
            di = turn_order(s)[place]
            back.send(
                q * 15 + di, parts.at[q, at(q, di, 2)], ra.at[q, di], {"req": at(q, 0, s)}
            )
            back.send(
                q * 15 + 4 + di, parts.at[q, at(q, di, -s)], rb.at[q, di], {"req": at(q, 0, -s)}
            )
    for place in range(4):
        for q, (_, s) in enumerate(TURNS):
            di = turn_order(s)[place]
            back.arrived(q * 15 + di)
            add(q, di, s, ra[q, di])
            back.send(
                q * 15 + 8 + di, parts.at[q, at(q, di, s)], rc.at[q, di], {"req": at(q, 0, s)}
            )
    for place in range(4):
        for q, (_, s) in enumerate(TURNS):
            di = turn_order(s)[place]
            back.arrived(q * 15 + 4 + di)
            back.arrived(q * 15 + 8 + di)
            add(q, di, 0, rb[q, di], rc[q, di])
            if place == 0:
                back.send(q * 15 + 12, parts.at[q, at(q, 2, 0)], rd.at[q], {"req": at(q, s, 0)})
            if place == 1:
                back.send(q * 15 + 13, parts.at[q, at(q, -s, 0)], re.at[q], {"req": at(q, -s, 0)})
    for q, (_, s) in enumerate(TURNS):
        back.arrived(q * 15 + 12)
        add(q, s, 0, rd[q])
        back.send(q * 15 + 14, parts.at[q, at(q, s, 0)], rf.at[q], {"req": at(q, s, 0)})
    for q in range(4):
        back.arrived(q * 15 + 13)
        back.arrived(q * 15 + 14)
        total = parts[q, r].astype(F32) + re[q].astype(F32) + rf[q].astype(F32)
        eo[q] = total.astype(BF16)

    weight = gate_r[:, 0:1]
    for q in range(4):
        cols = slice(q * QUARTER, (q + 1) * QUARTER)
        out = dot_nn(dispt_r[...], eo[q]) * weight
        for b in range(8):
            blocks[b % 2, b // 2, :, cols] = out[b * 32 : (b + 1) * 32, :].astype(BF16)
    last = Sender(head_send, head_recv)
    halves = reduce_over_head(blocks, got, relay, near, far, sent, last, 0)
    for q in range(2):
        cols = slice(q * HALF, (q + 1) * HALF)
        layer_r[:, cols] = (resid_r[:, cols].astype(F32) + halves[q]).astype(BF16)
    sender.drain()
    back.drain()
    last.drain()


def ffn_stage(args):
    vmem = pl.BlockSpec(memory_space=pltpu.VMEM)
    anywhere = pl.BlockSpec(memory_space=pl.ANY)
    block = (CAP, QUARTER)
    return pl.pallas_call(
        ffn_kernel,
        out_shape=jax.ShapeDtypeStruct((32, 2048), BF16),
        in_specs=[vmem] * 4 + [anywhere] * 2,
        out_specs=vmem,
        scratch_shapes=[
            pltpu.VMEM((4, 16) + block, BF16),
            pltpu.VMEM((4, 16) + block, BF16),
            pltpu.VMEM((4, 4) + block, BF16),
            pltpu.VMEM((4, 4) + block, BF16),
            pltpu.VMEM((4, 4) + block, BF16),
            pltpu.VMEM((4,) + block, BF16),
            pltpu.VMEM((4,) + block, BF16),
            pltpu.VMEM((4,) + block, BF16),
            pltpu.VMEM((2, 352, 2048), BF16),
            pltpu.VMEM((352, 2048), BF16),
            pltpu.VMEM((4,) + block, BF16),
            pltpu.VMEM((2, 4, 32, 2048), BF16),
        ]
        + HEAD_SCRATCH
        + [
            pltpu.SemaphoreType.DMA((2,)),
            pltpu.SemaphoreType.DMA((LAST,)),
            pltpu.SemaphoreType.DMA((LAST,)),
            pltpu.SemaphoreType.DMA((LAST,)),
            pltpu.SemaphoreType.DMA((LAST,)),
            pltpu.SemaphoreType.DMA((10,)),
            pltpu.SemaphoreType.DMA((10,)),
        ],
        compiler_params=pltpu.CompilerParams(collective_id=2, has_side_effects=True),
        name="ffn_stage",
    )(*args)


def on_device(
    hidden,
    attn_gain,
    attn_router,
    attention_expert_pairs,
    key_value_weight,
    query_weight,
    output_weight,
    paged_key_value_cache,
    page_table,
    cache_len,
    ancestor,
    ffn_gain,
    ffn_router,
    ffn_route,
    w_gate_up,
    w_down,
    accept_path,
    accept_count,
    mig_slot,
    destination,
):
    route = ffn_route.T
    part, mover, disp, dispt, pool = attend(
        (
            cache_len,
            page_table,
            accept_count,
            mig_slot,
            hidden,
            attn_gain.reshape(1, -1),
            attn_router.T,
            attention_expert_pairs.T,
            ancestor,
            accept_path,
            route,
            key_value_weight,
            query_weight,
            output_weight,
            paged_key_value_cache,
        )
    )
    outb, resid, gate, incoming = head_stage(
        (
            destination,
            part,
            hidden,
            ffn_gain.reshape(1, -1),
            ffn_router.T,
            route,
            mover,
            disp,
        )
    )
    layer_out = ffn_stage((outb, resid, gate, dispt, w_gate_up[0], w_down[0]))
    pool = lax.dynamic_update_slice(pool, incoming, (0, ENTRIES, 0, 0))
    return (layer_out, pool)


def solution(mesh):
    return jax.shard_map(
        on_device,
        mesh=mesh,
        in_specs=(
            P("req", None),
            P(),
            P(),
            P("req", None),
            P(None, None, "head"),
            P(None, None, "head"),
            P(None, "head", None),
            P(None, "req", None, "head"),
            P("req", None),
            P("req"),
            P("req", None, None),
            P(),
            P(),
            P("req", None),
            P("head", None, "req", None),
            P("head", "req", None),
            P("req", None),
            P("req"),
            P("req"),
            P(),
        ),
        out_specs=(P(("req", "head"), None), P(None, "req", None, "head")),
        check_vma=False,
    )
```

time: 486 us -> 146 us (0.30)
  waiting for transfers between devices: 270 us -> 0 us
  Pallas kernels: 0 us -> 142 us
  local copies, waits for them, and re-layouts: 89.2 us -> 2.29 us
  matrix products: 64.3 us -> 0 us
  other arithmetic: 36.7 us -> 0 us
  between operations: 17.2 us -> 1.32 us
  starting transfers between devices: 5.81 us -> 0 us
    psum x2 -> x0, waiting for transfers between devices: 187 us -> none  [the longest x1 120 us: on_device(): lax.psum(partial_all.astype(jnp.bfloat16), 'req').astype(jnp.float32)]
    pallas_call x0 -> x3, Pallas kernels: none -> 142 us  [the longest x1 95.5 us: ffn_stage(): pl.pallas_call(ffn_kernel, out_shape=jax.ShapeDtypeStruct((32, 2048), BF1...]
    dot_general x17 -> x0, matrix products: 64.3 us -> none  [the longest x2 24 us: on_device(): jnp.dot(prob_c, stored_value_rows, preferred_element_type=jnp.float32)]
    all_gather x1 -> x0, waiting for transfers between devices: 62.4 us -> none  [on_device(): lax.all_gather(outbound, 'req', axis=0, tiled=True)]
    gather x19 -> x0, local copies, waits for them, and re-layouts: 23 us -> none  [the longest x8 9.08 us: pair_gates(): picked = jnp.take_along_axis(logits, route_ids, axis=1)]
    reshape x8 -> x0, local copies, waits for them, and re-layouts: 21 us -> none  [the longest x1 12.5 us: on_device(): valid_cache = jnp.repeat(valid_cache, 2, axis=0)]
    reduce_scatter x1 -> x0, waiting for transfers between devices: 20.4 us -> none  [on_device(): lax.psum_scatter(ffn_part.astype(jnp.bfloat16), 'head', scatter_dimension...]
    reduce_sum x9 -> x0, other arithmetic: 12.8 us -> none  [the longest x1 5.86 us: on_device(): jnp.sum(exp_c, axis=1, keepdims=True)]
  transfers between devices with their start and end apart: 5 -> 0, of which waited for: 4 -> 0; matrix products, arithmetic and copies ran while one was open for 9% -> 0% of each run, Pallas kernels for 0% -> 0%
where the time goes in v1:
time: 146 us
  Pallas kernels  142 us (97%)
  local copies, waits for them, and re-layouts  2.29 us (2%)
    pallas_call x1, Pallas kernels, ffn_stage(): pl.pallas_call(ffn_kernel, out_shape=jax.ShapeDtypeStruct((32, 2048), BF1...  95.5 us
    pallas_call x1, Pallas kernels, head_stage(): pl.pallas_call(head_kernel, out_shape=(jax.ShapeDtypeStruct((4, CAP, QUAR...  29 us
    pallas_call x1, Pallas kernels, attend(): pl.pallas_call(attend_kernel, out_shape=(jax.ShapeDtypeStruct((2, 4, 32,...  17.5 us

profile of v1, /device:TPU:1, one launch (start us, length us, event | category | flops | bytes accessed | tf_op | source)
XLA Modules:
  0.0 145.6 jit_solution(8138408189570600515)
XLA Ops:
  1.3 17.5 %attend.1 = (bf16[2,4,32,2048]{3,2,1,0:T(8,128)(2,1)}, bf16[2,2,128,256]{3,2,1,0:T(8,128)(2,1)}, bf16[96,256]{1,0:T(8,128)(2,1)}, bf16[256,96]{1,0:T(8,128)(2,1)}, bf16[2,32,128,256]{3,2,1,0:T(8,128)(2,1)}) custom-call(s32[4]{0:T(128)} %len_s.1, s32[4,30]{1,0:T(4,128)} %table_s.1, s32[4]{0:T(128)} %count_s.1, s32[1]{0:T(128)S(6)} %copy.24.mig_s, ...), custom_call_target="tpu_custom_call" | custom-call | tf_op jit(solution)/shard_map/attend/pallas_call | solution.py:306
  18.8 29.0 %head_stage.1 = (bf16[4,96,512]{2,1,0:T(8,128)(2,1)}, bf16[32,2048]{1,0:T(8,128)(2,1)}, f32[256,128]{1,0:T(8,128)}, bf16[2,2,128,256]{3,2,1,0:T(8,128)(2,1)}) custom-call(s32[16]{0:T(128)} %dest_s.1, bf16[2,4,32,2048]{3,2,1,0:T(8,128)(2,1)} %get-tuple-element.11.part_r, bf16[256,2048]{1,0:T(8,128)(2,1)} %hidden_r.3, f32[1,2048]{1,0:T(1,128)} %bitcast.13, ...), custom_call_target="tpu_custom_call" | custom-call | tf_op jit(solution)/shard_map/head_stage/pallas_call | solution.py:563
  47.8 0.0 copy-start
  47.8 95.5 %ffn_stage.1 = bf16[32,2048]{1,0:T(8,128)(2,1)} custom-call(bf16[4,96,512]{2,1,0:T(8,128)(2,1)} %get-tuple-element.14.outb_r, bf16[32,2048]{1,0:T(8,128)(2,1)} %get-tuple-element.15.resid_r, f32[256,128]{1,0:T(8,128)} %get-tuple-element.16.gate_r, bf16[256,96]{1,0:T(8,128)(2,1)} %get-tuple-element.17.dispt_r, bf16[2,352,2048]{2,1,0:T(8,128)(2,1)} %bitcast.8, ...), custom_call_target="tpu_custom_call" | custom-call | tf_op jit(solution)/shard_map/ffn_stage/pallas_call | solution.py:786
  143.3 0.0 copy-done
  143.3 0.7 constant_dynamic-update-slice_fusion
  144.1 1.6 %copy.25 = bf16[32,2048]{1,0:T(8,128)(2,1)} copy(bf16[32,2048]{1,0:T(8,128)(2,1)} %ffn_stage.1) | data formatting | bytes 262144
Async XLA Ops:
  47.8 95.5 %copy-start = (bf16[2,2,128,256]{3,2,1,0:T(8,128)(2,1)S(1)}, bf16[2,2,128,256]{3,2,1,0:T(8,128)(2,1)}, u32[]{:S(2)}) copy-start(bf16[2,2,128,256]{3,2,1,0:T(8,128)(2,1)} %get-tuple-element.19) | copy-start | bytes 786436
